TPU v7x, 512 devices: a whole 4x8x8 slice. The times are simulated.
512 devices in a mesh: dp: 4 (over z_hi), loop: 128 (over x, y, z_lo, core).
Axes of the slice: x: 4, y: 8, z: 8 (z_hi: 4, z_lo: 2; z = z_hi * 2 + z_lo), core: 2. Of those that a mesh axis runs over, the one named last changes fastest.
Arguments:
- tokens: bfloat16 [8192, 2048], P('loop', 'dp'), may hold values from -6 to 6
- cotangent: bfloat16 [8192, 2048], P('loop', 'dp'), may hold values from -6 to 6
- up_first: bfloat16 [128, 256, 128], P('loop'), may hold values from -0.5 to 0.5
- up_second: bfloat16 [256, 128, 128], P('loop'), may hold values from -0.5 to 0.5
- down_first: bfloat16 [256, 128, 128], P('loop'), may hold values from -0.5 to 0.5
- down_second: bfloat16 [128, 256, 128], P('loop'), may hold values from -0.25 to 0.25
- perm_up: int32 [128], replicated, may hold values from 0 to 127, each once
- perm_down: int32 [128], replicated, may hold values from 0 to 127, each once
Outputs:
- mixed: bfloat16 [8192, 2048], P('loop', 'dp')
- grad_tokens: bfloat16 [8192, 2048], P('loop', 'dp')
- grad_up_first: float32 [128, 256, 128], P('loop')
- grad_up_second: float32 [256, 128, 128], P('loop')
- grad_down_first: float32 [256, 128, 128], P('loop')
- grad_down_second: float32 [128, 256, 128], P('loop')
Inputs may be any that keep to these rules, and one draw needn't show every extreme that they name: perm_up holds each of 0 to 127 once. perm_down holds each of 0 to 127 once.
All inputs are finite; a program needn't handle non-finite values.
Results may differ from a plain program's by a relative error of at most 0.01.
Values may be sent and summed in bfloat16 or wider, within the bound.
A program may use at most 64 MiB of HBM per device.

v0:
```python
import math

import jax
import jax.numpy as jnp
from jax import lax
from jax.sharding import Mesh
from jax.sharding import PartitionSpec as P

LOOP = ("loop_0", "loop_1", "loop_2", "loop_3")


def from_partner(value, axis, apart):
    mask = 2**apart
    pairs = [(source, source ^ mask) for source in range(lax.axis_size(axis))]
    return lax.ppermute(value, axis, pairs)


def split_up(array, dim, count):
    lengths = array.shape
    tiles = array.reshape(*lengths[:dim], count, lengths[dim] // count, *lengths[dim + 1 :])
    return jnp.moveaxis(tiles, dim, 0)


def laid_out(tiles, dim):
    tiles = jnp.moveaxis(tiles, 0, dim)
    lengths = tiles.shape
    return tiles.reshape(*lengths[:dim], lengths[dim] * lengths[dim + 1], *lengths[dim + 2 :])


def turned_blocks(tiles, axes, sequence):
    lengths = [lax.axis_size(a) for a in axes]
    tiles = tiles.reshape(*lengths, *tiles.shape[1:])
    for k in sequence:
        tiles = lax.all_to_all(tiles, axes[k], split_axis=k, concat_axis=k, tiled=True)
    return tiles.reshape(-1, *tiles.shape[len(axes) :])


def core_and_chips(array, groups, sequence, split_dim, concat_dim):
    count = lax.axis_size(groups[0]) * lax.axis_size(groups[1])
    tiles = split_up(array, split_dim, count)
    return laid_out(turned_blocks(tiles, groups, sequence), concat_dim)


def from_everyone(array, axis):
    count = lax.axis_size(axis)
    return lax.all_to_all(
        jnp.broadcast_to(array[None], (count, *array.shape)), axis, 0, 0, tiled=True
    )


def taken_together(array, axis):
    return from_everyone(array, axis).astype(jnp.float32).sum(axis=0)


def gelu_parts(pre_act):
    cumul = 0.5 * (1.0 + jax.scipy.special.erf(pre_act * (1.0 / math.sqrt(2.0))))
    slope = cumul + pre_act * jnp.exp(-0.5 * pre_act * pre_act) * (1.0 / math.sqrt(2.0 * math.pi))
    return (pre_act * cumul, slope)


def inverse_of(permute):
    return (
        jnp.zeros(permute.shape, jnp.int32)
        .at[permute]
        .set(jnp.arange(permute.shape[0], dtype=jnp.int32))
    )


def pair_total(contrib, half_width, parity):
    pair_blocks = contrib.shape[0]
    tok_count = contrib.shape[2]
    leaving = lax.dynamic_slice_in_dim(contrib, (1 - parity) * half_width, half_width, 1)
    other = from_partner(leaving.astype(jnp.bfloat16), LOOP, 0).astype(leaving.dtype)
    mine = lax.dynamic_slice_in_dim(contrib, parity * half_width, half_width, 1) + other
    return mine.reshape(pair_blocks * half_width, tok_count)


def shards(tokens, cotangent, up_first, up_second, down_first, down_second, perm_up, perm_down):
    wide = jnp.float32
    narrow = jnp.bfloat16
    feature_rows = tokens.shape[0]
    tok_count = tokens.shape[1]
    local_rows = up_first.shape[0]
    block = up_first.shape[2]
    half_width = block // 2
    pair_blocks = 2 * feature_rows // block
    group = 2 * local_rows // pair_blocks
    parity = lax.axis_index(LOOP) % 2
    other_x, other_d = from_partner((tokens, cotangent), LOOP, 0)
    low_x = jnp.where(parity == 0, tokens, other_x)
    high_x = jnp.where(parity == 0, other_x, tokens)
    low_d = jnp.where(parity == 0, cotangent, other_d)
    high_d = jnp.where(parity == 0, other_d, cotangent)
    x_blocks = jnp.concatenate(
        [
            low_x.reshape(pair_blocks, half_width, tok_count),
            high_x.reshape(pair_blocks, half_width, tok_count),
        ],
        1,
    )
    d_blocks = jnp.concatenate(
        [
            low_d.reshape(pair_blocks, half_width, tok_count),
            high_d.reshape(pair_blocks, half_width, tok_count),
        ],
        1,
    )
    row_block = (parity * local_rows + jnp.arange(local_rows, dtype=jnp.int32)) // group
    picker = row_block[:, None] == jnp.arange(pair_blocks, dtype=jnp.int32)[None, :]
    picker_narrow = picker.astype(narrow)
    picker_wide = picker.astype(wide)
    x_rows = jnp.einsum("am,mit->ait", picker_narrow, x_blocks, preferred_element_type=wide).astype(
        narrow
    )
    d_rows = jnp.einsum("am,mit->ait", picker_narrow, d_blocks, preferred_element_type=wide).astype(
        narrow
    )
    inverse_up = inverse_of(perm_up)
    inverse_down = inverse_of(perm_down)
    hidden_one = jnp.einsum("abi,ait->abt", up_first, x_rows, preferred_element_type=wide).astype(
        narrow
    )
    permuted = jnp.take(
        core_and_chips(hidden_one, (("loop_0", "loop_1", "loop_2"), "loop_3"), (1, 0), 1, 0),
        perm_up,
        axis=0,
    )
    pre_act = jnp.einsum("boa,abt->bot", up_second, permuted, preferred_element_type=wide)
    gelu_val, slope = gelu_parts(pre_act)
    activated = gelu_val.astype(narrow)
    mixed_cols = jnp.einsum(
        "bpo,bot->pbt", down_first, activated, preferred_element_type=wide
    ).astype(narrow)
    leaving = jnp.take(mixed_cols, perm_down, axis=0)
    back_rows = lax.all_to_all(leaving, LOOP, split_axis=0, concat_axis=1, tiled=True)
    back_rows, permuted, activated, slope = (back_rows, permuted, activated, slope)
    out_rows = jnp.einsum("abo,abt->aot", down_second, back_rows, preferred_element_type=wide)
    out_contrib = jnp.einsum("am,aot->mot", picker_wide, out_rows, precision=lax.Precision.HIGHEST)
    branch_out = pair_total(out_contrib, half_width, parity)
    mixed = (tokens.astype(wide) + branch_out).astype(narrow)
    scale = 1.0 / math.sqrt(lax.axis_size("dp") * tok_count)
    grad_rows = jnp.einsum("abo,aot->abt", down_second, d_rows, preferred_element_type=wide).astype(
        narrow
    )
    g_down_second = jnp.einsum("abt,aot->abo", back_rows, d_rows, preferred_element_type=wide)
    grad_cols = lax.all_to_all(grad_rows, LOOP, split_axis=1, concat_axis=0, tiled=True)
    grad_mixed = jnp.take(grad_cols, inverse_down, axis=0)
    grad_act = jnp.einsum("bpo,pbt->bot", down_first, grad_mixed, preferred_element_type=wide)
    g_down_first = jnp.einsum("pbt,bot->bpo", grad_mixed, activated, preferred_element_type=wide)
    grad_pre = (grad_act * slope).astype(narrow)
    g_up_second = jnp.einsum("bot,abt->boa", grad_pre, permuted, preferred_element_type=wide)
    grad_perm = jnp.einsum("boa,bot->abt", up_second, grad_pre, preferred_element_type=wide).astype(
        narrow
    )
    grad_recv = jnp.take(grad_perm, inverse_up, axis=0)
    grad_hidden = lax.all_to_all(grad_recv, LOOP, split_axis=0, concat_axis=1, tiled=True)
    g_up_first = jnp.einsum("abt,ait->abi", grad_hidden, x_rows, preferred_element_type=wide)
    g_up_first, g_up_second, g_down_first, g_down_second = (
        taken_together(g_up_first.astype(jnp.bfloat16), "dp").astype(jnp.float32),
        taken_together(g_up_second.astype(jnp.bfloat16), "dp").astype(jnp.float32),
        taken_together(g_down_first.astype(jnp.bfloat16), "dp").astype(jnp.float32),
        taken_together(g_down_second.astype(jnp.bfloat16), "dp").astype(jnp.float32),
    )
    grad_rows_in = jnp.einsum("abi,abt->ait", up_first, grad_hidden, preferred_element_type=wide)
    grad_contrib = jnp.einsum(
        "am,ait->mit", picker_wide, grad_rows_in, precision=lax.Precision.HIGHEST
    )
    grad_branch = pair_total(grad_contrib, half_width, parity)
    grad_tokens = (cotangent.astype(wide) + grad_branch).astype(narrow)
    return (
        mixed,
        grad_tokens,
        g_up_first * scale,
        g_up_second * scale,
        g_down_first * scale,
        g_down_second * scale,
    )


def solution(mesh):
    split = Mesh(
        mesh.devices.reshape(mesh.shape["dp"], 4, 8, 2, 2),
        ("dp", "loop_0", "loop_1", "loop_2", "loop_3"),
    )
    placed = (
        P(LOOP, "dp"),
        P(LOOP, "dp"),
        P(LOOP, None, None),
        P(LOOP, None, None),
        P(LOOP, None, None),
        P(LOOP, None, None),
        P(),
        P(),
    )
    return jax.shard_map(
        shards,
        mesh=split,
        in_specs=placed,
        out_specs=(
            P(LOOP, "dp"),
            P(LOOP, "dp"),
            P(LOOP, None, None),
            P(LOOP, None, None),
            P(LOOP, None, None),
            P(LOOP, None, None),
        ),
        check_vma=False,
    )
```

profile of v0, /device:TPU:6, one launch (start us, length us, event | category | flops | bytes accessed | tf_op | source)
XLA Modules:
  0.0 167.1 jit_solution(2929654481980371167)
XLA Ops:
  0.7 2.1 %collective-permute-start = (bf16[64,512]{1,0:T(8,128)(2,1)}, bf16[64,512]{1,0:T(8,128)(2,1)S(1)}, u32[]{:S(2)}, u32[]{:S(2)}) collective-permute-start(bf16[64,512]{1,0:T(8,128)(2,1)} %param.10), channel_id=1, source_target_pairs={{0,1},{1,0},{2,3},{3,2},{4,5},{5,4},{6,7},{7,6},{8,9},{9,8},{10,11... | collective-permute-start | bytes 196616 | tf_op jit(solution)/shard_map/ppermute | solution.py:15
  2.7 2.4 %collective-permute-start.2 = (bf16[64,512]{1,0:T(8,128)(2,1)}, bf16[64,512]{1,0:T(8,128)(2,1)S(1)}, u32[]{:S(2)}, u32[]{:S(2)}) collective-permute-start(bf16[64,512]{1,0:T(8,128)(2,1)} %param.11), channel_id=1, source_target_pairs={{0,1},{1,0},{2,3},{3,2},{4,5},{5,4},{6,7},{7,6},{8,9},{9,8},{10,11... | collective-permute-start | bytes 196616 | tf_op jit(solution)/shard_map/ppermute | solution.py:15
  5.2 0.6 copy-done.6
  5.8 0.6 copy-done.7
  6.5 1.0 scatter_custom_fusion.1
  7.5 1.0 scatter_custom_fusion
  8.6 0.8 copy-done.4
  9.9 3.9 %all_to_all.60 = bf16[64,2,1,2,512]{4,3,0,2,1:T(2,128)(2,1)S(1)} all-to-all(bf16[64,2,1,2,512]{4,3,0,2,1:T(2,128)(2,1)S(1)} %copy.38), channel_id=1, replica_groups=mesh['dp'=4,'loop_0'=4,'loop_1'=8,'loop_2'=2,'loop_3'=2] {'loop_3'}, dimensions={1} | all-to-all | bytes 524288 | tf_op jit(solution)/shard_map/all_to_all | solution.py:34
  13.9 0.9 copy.39
  14.8 12.7 %all-to-all-start.1 = ((bf16[64,2,1,2,512]{4,3,1,2,0:T(2,128)(2,1)}), bf16[64,2,1,2,512]{4,3,1,2,0:T(2,128)(2,1)S(1)}, u32[]{:S(2)}, u32[]{:S(2)}) async-start(bf16[64,2,1,2,512]{4,3,1,2,0:T(2,128)(2,1)} %copy.39), calls=%async_computation.1 | async-start | bytes 524288 | tf_op jit(solution)/shard_map/all_to_all | solution.py:34
  27.6 0.8 copy-done.3
  29.1 0.5 broadcast.80
  29.6 2.2 %reduce.4 = bf16[256,512]{1,0:T(8,128)(2,1)S(1)} reduce(bf16[256,1,512]{2,1,0:T(2,128)(2,1)S(1)} %bitcast.108, bf16[]{:T(256)} %broadcast.80), dimensions={1}, to_apply=%bitcast.91.reduce_sub_computation | reduce | bytes 524290
  31.9 0.8 reshape.236
  32.7 6.5 %all-to-all-done.1 = bf16[64,2,1,2,512]{4,3,1,2,0:T(2,128)(2,1)S(1)} async-done(((bf16[64,2,1,2,512]{4,3,1,2,0:T(2,128)(2,1)}), bf16[64,2,1,2,512]{4,3,1,2,0:T(2,128)(2,1)S(1)}, u32[]{:S(2)}, u32[]{:S(2)}) %all-to-all-start.1) | async-done | bytes 262176 | tf_op jit(solution)/shard_map/all_to_all | solution.py:34
  39.2 7.8 %all-to-all-start.3 = ((bf16[128,2,512]{2,1,0:T(2,128)(2,1)}), bf16[128,2,512]{2,1,0:T(2,128)(2,1)S(1)}, u32[]{:S(2)}, u32[]{:S(2)}) async-start(bf16[128,2,512]{2,1,0:T(2,128)(2,1)} %reshape.236), calls=%async_computation.3 | async-start | bytes 524288 | tf_op jit(solution)/shard_map/all_to_all | solution.py:146
  47.0 1.1 gather_fusion
  49.8 1.1 gather_fusion.1
  50.9 7.6 %all-to-all-done.3 = bf16[128,2,512]{2,1,0:T(2,128)(2,1)S(1)} async-done(((bf16[128,2,512]{2,1,0:T(2,128)(2,1)}), bf16[128,2,512]{2,1,0:T(2,128)(2,1)S(1)}, u32[]{:S(2)}, u32[]{:S(2)}) %all-to-all-start.3) | async-done | bytes 262176 | tf_op jit(solution)/shard_map/all_to_all | solution.py:146
  58.7 1.5 bitcast_reduce_fusion
  60.3 1.1 gather_fusion.2
  62.4 0.7 broadcast_in_dim.24
  63.1 9.4 %all-to-all-start.6 = ((bf16[4,2,128,128]{3,2,1,0:T(8,128)(2,1)}), bf16[4,2,128,128]{3,2,1,0:T(8,128)(2,1)S(1)}, u32[]{:S(2)}, u32[]{:S(2)}) async-start(bf16[4,2,128,128]{3,2,1,0:T(8,128)(2,1)} %broadcast_in_dim.24), calls=%async_computation.6 | async-start | bytes 524288 | tf_op jit(solution)/shard_map/all_to_all | solution.py:46
  72.5 1.0 broadcast_select_fusion.2
  73.8 9.5 %all-to-all-done.6 = bf16[4,2,128,128]{3,2,1,0:T(8,128)(2,1)S(1)} async-done(((bf16[4,2,128,128]{3,2,1,0:T(8,128)(2,1)}), bf16[4,2,128,128]{3,2,1,0:T(8,128)(2,1)S(1)}, u32[]{:S(2)}, u32[]{:S(2)}) %all-to-all-start.6) | async-done | bytes 262176 | tf_op jit(solution)/shard_map/all_to_all | solution.py:46
  83.3 0.7 broadcast_in_dim.44
  84.0 3.4 %all-to-all-start.7 = ((bf16[4,2,128,128]{3,2,1,0:T(8,128)(2,1)}), bf16[4,2,128,128]{3,2,1,0:T(8,128)(2,1)S(1)}, u32[]{:S(2)}, u32[]{:S(2)}) async-start(bf16[4,2,128,128]{3,2,1,0:T(8,128)(2,1)} %broadcast_in_dim.44), calls=%async_computation.7 | async-start | bytes 524288 | tf_op jit(solution)/shard_map/all_to_all | solution.py:46
  87.8 1.1 gather_fusion.3
  89.0 1.0 broadcast_select_fusion
  90.0 7.4 %all-to-all-done.7 = bf16[4,2,128,128]{3,2,1,0:T(8,128)(2,1)S(1)} async-done(((bf16[4,2,128,128]{3,2,1,0:T(8,128)(2,1)}), bf16[4,2,128,128]{3,2,1,0:T(8,128)(2,1)S(1)}, u32[]{:S(2)}, u32[]{:S(2)}) %all-to-all-start.7) | async-done | bytes 262176 | tf_op jit(solution)/shard_map/all_to_all | solution.py:46
  97.4 8.2 %all-to-all-start.2 = ((bf16[128,2,512]{2,1,0:T(2,128)(2,1)}), bf16[128,2,512]{2,1,0:T(2,128)(2,1)S(1)}, u32[]{:S(2)}, u32[]{:S(2)}) async-start(bf16[128,2,512]{2,1,0:T(2,128)(2,1)} %broadcast_select_fusion.2), calls=%async_computation.2 | async-start | bytes 524288 | tf_op jit(solution)/shard_map/all_to_all | solution.py:135
  105.6 0.7 broadcast_multiply_fusion.1
  106.3 0.7 broadcast_multiply_fusion
  107.0 10.1 %all-to-all-done.2 = bf16[128,2,512]{2,1,0:T(2,128)(2,1)S(1)} async-done(((bf16[128,2,512]{2,1,0:T(2,128)(2,1)}), bf16[128,2,512]{2,1,0:T(2,128)(2,1)S(1)}, u32[]{:S(2)}, u32[]{:S(2)}) %all-to-all-start.2) | async-done | bytes 262176 | tf_op jit(solution)/shard_map/all_to_all | solution.py:135
  117.0 8.4 %all-to-all-start.4 = ((bf16[128,2,512]{2,1,0:T(2,128)(2,1)}), bf16[128,2,512]{2,1,0:T(2,128)(2,1)S(1)}, u32[]{:S(2)}, u32[]{:S(2)}) async-start(bf16[128,2,512]{2,1,0:T(2,128)(2,1)} %broadcast_select_fusion), calls=%async_computation.4 | async-start | bytes 524288 | tf_op jit(solution)/shard_map/all_to_all | solution.py:156
  125.8 2.0 %collective-permute-start.1 = (bf16[1,64,512]{2,1,0:T(8,128)(2,1)S(1)}, bf16[1,64,512]{2,1,0:T(8,128)(2,1)S(1)}, u32[]{:S(2)}, u32[]{:S(2)}) collective-permute-start(bf16[1,64,512]{2,1,0:T(8,128)(2,1)S(1)} %fusion.26), channel_id=1, source_target_pairs={{0,1},{1,0},{2,3},{3,2},{4,5},{5,4},{6,7},{7,6},{8,9},{9,8},{10,11... | collective-permute-start | bytes 196616 | tf_op jit(solution)/shard_map/ppermute | solution.py:15
  128.1 8.8 %all-to-all-done.4 = bf16[128,2,512]{2,1,0:T(2,128)(2,1)S(1)} async-done(((bf16[128,2,512]{2,1,0:T(2,128)(2,1)}), bf16[128,2,512]{2,1,0:T(2,128)(2,1)S(1)}, u32[]{:S(2)}, u32[]{:S(2)}) %all-to-all-start.4) | async-done | bytes 262176 | tf_op jit(solution)/shard_map/all_to_all | solution.py:156
  136.9 0.7 broadcast_in_dim.45
  137.6 3.4 %all-to-all-start.8 = ((bf16[4,1,256,128]{3,2,1,0:T(8,128)(2,1)}), bf16[4,1,256,128]{3,2,1,0:T(8,128)(2,1)S(1)}, u32[]{:S(2)}, u32[]{:S(2)}) async-start(bf16[4,1,256,128]{3,2,1,0:T(8,128)(2,1)} %broadcast_in_dim.45), calls=%async_computation.8 | async-start | bytes 524288 | tf_op jit(solution)/shard_map/all_to_all | solution.py:46
  141.6 2.1 %collective-permute-start.3 = (bf16[1,64,512]{2,1,0:T(8,128)(2,1)S(1)}, bf16[1,64,512]{2,1,0:T(8,128)(2,1)S(1)}, u32[]{:S(2)}, u32[]{:S(2)}) collective-permute-start(bf16[1,64,512]{2,1,0:T(8,128)(2,1)S(1)} %fusion.27), channel_id=1, source_target_pairs={{0,1},{1,0},{2,3},{3,2},{4,5},{5,4},{6,7},{7,6},{8,9},{9,8},{10,11... | collective-permute-start | bytes 196616 | tf_op jit(solution)/shard_map/ppermute | solution.py:15
  143.7 0.7 fusion.21
  144.4 7.6 %all-to-all-done.8 = bf16[4,1,256,128]{3,2,1,0:T(8,128)(2,1)S(1)} async-done(((bf16[4,1,256,128]{3,2,1,0:T(8,128)(2,1)}), bf16[4,1,256,128]{3,2,1,0:T(8,128)(2,1)S(1)}, u32[]{:S(2)}, u32[]{:S(2)}) %all-to-all-start.8) | async-done | bytes 262176 | tf_op jit(solution)/shard_map/all_to_all | solution.py:46
  152.0 0.7 broadcast_in_dim.23
  152.8 3.4 %all-to-all-start.5 = ((bf16[4,1,256,128]{3,2,1,0:T(8,128)(2,1)}), bf16[4,1,256,128]{3,2,1,0:T(8,128)(2,1)S(1)}, u32[]{:S(2)}, u32[]{:S(2)}) async-start(bf16[4,1,256,128]{3,2,1,0:T(8,128)(2,1)} %broadcast_in_dim.23), calls=%async_computation.5 | async-start | bytes 524288 | tf_op jit(solution)/shard_map/all_to_all | solution.py:46
  156.2 0.7 fusion.18
  156.9 0.7 multiply_bitcast_fusion
  157.6 8.8 %all-to-all-done.5 = bf16[4,1,256,128]{3,2,1,0:T(8,128)(2,1)S(1)} async-done(((bf16[4,1,256,128]{3,2,1,0:T(8,128)(2,1)}), bf16[4,1,256,128]{3,2,1,0:T(8,128)(2,1)S(1)}, u32[]{:S(2)}, u32[]{:S(2)}) %all-to-all-start.5) | async-done | bytes 262176 | tf_op jit(solution)/shard_map/all_to_all | solution.py:46
  166.4 0.7 multiply_bitcast_fusion.1
  (59 shorter events, 6.1 us)
Async XLA Ops:
  0.6 47.9 %copy-start = (bf16[2,128,128]{2,1,0:T(8,128)(2,1)S(1)}, bf16[2,128,128]{2,1,0:T(8,128)(2,1)}, u32[]{:S(2)}) copy-start(bf16[2,128,128]{2,1,0:T(8,128)(2,1)} %param.13) | copy-start | bytes 196612
  0.6 7.9 %copy-start.1 = (bf16[64,512]{1,0:T(8,128)(2,1)S(1)}, bf16[64,512]{1,0:T(8,128)(2,1)}, u32[]{:S(2)}) copy-start(bf16[64,512]{1,0:T(8,128)(2,1)} %param.10) | copy-start | bytes 196612
  0.7 7.9 %collective-permute-start = (bf16[64,512]{1,0:T(8,128)(2,1)}, bf16[64,512]{1,0:T(8,128)(2,1)S(1)}, u32[]{:S(2)}, u32[]{:S(2)}) collective-permute-start(bf16[64,512]{1,0:T(8,128)(2,1)} %param.10), channel_id=1, source_target_pairs={{0,1},{1,0},{2,3},{3,2},{4,5},{5,4},{6,7},{7,6},{8,9},{9,8},{10,11... | collective-permute-start | bytes 196616 | tf_op jit(solution)/shard_map/ppermute | solution.py:15
  2.7 24.9 %collective-permute-start.2 = (bf16[64,512]{1,0:T(8,128)(2,1)}, bf16[64,512]{1,0:T(8,128)(2,1)S(1)}, u32[]{:S(2)}, u32[]{:S(2)}) collective-permute-start(bf16[64,512]{1,0:T(8,128)(2,1)} %param.11), channel_id=1, source_target_pairs={{0,1},{1,0},{2,3},{3,2},{4,5},{5,4},{6,7},{7,6},{8,9},{9,8},{10,11... | collective-permute-start | bytes 196616 | tf_op jit(solution)/shard_map/ppermute | solution.py:15
  5.2 0.7 copy-start.6
  5.8 0.7 copy-start.7
  8.6 0.8 copy-start.4
  14.8 12.8 %copy-start.2 = (bf16[64,512]{1,0:T(8,128)(2,1)S(1)}, bf16[64,512]{1,0:T(8,128)(2,1)}, u32[]{:S(2)}) copy-start(bf16[64,512]{1,0:T(8,128)(2,1)} %param.11) | copy-start | bytes 196612
  14.8 24.4 %all-to-all-start.1 = ((bf16[64,2,1,2,512]{4,3,1,2,0:T(2,128)(2,1)}), bf16[64,2,1,2,512]{4,3,1,2,0:T(2,128)(2,1)S(1)}, u32[]{:S(2)}, u32[]{:S(2)}) async-start(bf16[64,2,1,2,512]{4,3,1,2,0:T(2,128)(2,1)} %copy.39), calls=%async_computation.1 | async-start | bytes 524288 | tf_op jit(solution)/shard_map/all_to_all | solution.py:34
  27.6 0.8 copy-start.3
  39.2 19.3 %all-to-all-start.3 = ((bf16[128,2,512]{2,1,0:T(2,128)(2,1)}), bf16[128,2,512]{2,1,0:T(2,128)(2,1)S(1)}, u32[]{:S(2)}, u32[]{:S(2)}) async-start(bf16[128,2,512]{2,1,0:T(2,128)(2,1)} %reshape.236), calls=%async_computation.3 | async-start | bytes 524288 | tf_op jit(solution)/shard_map/all_to_all | solution.py:146
  48.5 0.8 copy-start.5
  63.1 20.1 %all-to-all-start.6 = ((bf16[4,2,128,128]{3,2,1,0:T(8,128)(2,1)}), bf16[4,2,128,128]{3,2,1,0:T(8,128)(2,1)S(1)}, u32[]{:S(2)}, u32[]{:S(2)}) async-start(bf16[4,2,128,128]{3,2,1,0:T(8,128)(2,1)} %broadcast_in_dim.24), calls=%async_computation.6 | async-start | bytes 524288 | tf_op jit(solution)/shard_map/all_to_all | solution.py:46
  84.0 13.4 %all-to-all-start.7 = ((bf16[4,2,128,128]{3,2,1,0:T(8,128)(2,1)}), bf16[4,2,128,128]{3,2,1,0:T(8,128)(2,1)S(1)}, u32[]{:S(2)}, u32[]{:S(2)}) async-start(bf16[4,2,128,128]{3,2,1,0:T(8,128)(2,1)} %broadcast_in_dim.44), calls=%async_computation.7 | async-start | bytes 524288 | tf_op jit(solution)/shard_map/all_to_all | solution.py:46
  97.4 19.6 %all-to-all-start.2 = ((bf16[128,2,512]{2,1,0:T(2,128)(2,1)}), bf16[128,2,512]{2,1,0:T(2,128)(2,1)S(1)}, u32[]{:S(2)}, u32[]{:S(2)}) async-start(bf16[128,2,512]{2,1,0:T(2,128)(2,1)} %broadcast_select_fusion.2), calls=%async_computation.2 | async-start | bytes 524288 | tf_op jit(solution)/shard_map/all_to_all | solution.py:135
  117.0 19.9 %all-to-all-start.4 = ((bf16[128,2,512]{2,1,0:T(2,128)(2,1)}), bf16[128,2,512]{2,1,0:T(2,128)(2,1)S(1)}, u32[]{:S(2)}, u32[]{:S(2)}) async-start(bf16[128,2,512]{2,1,0:T(2,128)(2,1)} %broadcast_select_fusion), calls=%async_computation.4 | async-start | bytes 524288 | tf_op jit(solution)/shard_map/all_to_all | solution.py:156
  125.8 17.9 %collective-permute-start.1 = (bf16[1,64,512]{2,1,0:T(8,128)(2,1)S(1)}, bf16[1,64,512]{2,1,0:T(8,128)(2,1)S(1)}, u32[]{:S(2)}, u32[]{:S(2)}) collective-permute-start(bf16[1,64,512]{2,1,0:T(8,128)(2,1)S(1)} %fusion.26), channel_id=1, source_target_pairs={{0,1},{1,0},{2,3},{3,2},{4,5},{5,4},{6,7},{7,6},{8,9},{9,8},{10,11... | collective-permute-start | bytes 196616 | tf_op jit(solution)/shard_map/ppermute | solution.py:15
  137.6 14.4 %all-to-all-start.8 = ((bf16[4,1,256,128]{3,2,1,0:T(8,128)(2,1)}), bf16[4,1,256,128]{3,2,1,0:T(8,128)(2,1)S(1)}, u32[]{:S(2)}, u32[]{:S(2)}) async-start(bf16[4,1,256,128]{3,2,1,0:T(8,128)(2,1)} %broadcast_in_dim.45), calls=%async_computation.8 | async-start | bytes 524288 | tf_op jit(solution)/shard_map/all_to_all | solution.py:46
  141.6 14.6 %collective-permute-start.3 = (bf16[1,64,512]{2,1,0:T(8,128)(2,1)S(1)}, bf16[1,64,512]{2,1,0:T(8,128)(2,1)S(1)}, u32[]{:S(2)}, u32[]{:S(2)}) collective-permute-start(bf16[1,64,512]{2,1,0:T(8,128)(2,1)S(1)} %fusion.27), channel_id=1, source_target_pairs={{0,1},{1,0},{2,3},{3,2},{4,5},{5,4},{6,7},{7,6},{8,9},{9,8},{10,11... | collective-permute-start | bytes 196616 | tf_op jit(solution)/shard_map/ppermute | solution.py:15
  152.8 13.6 %all-to-all-start.5 = ((bf16[4,1,256,128]{3,2,1,0:T(8,128)(2,1)}), bf16[4,1,256,128]{3,2,1,0:T(8,128)(2,1)S(1)}, u32[]{:S(2)}, u32[]{:S(2)}) async-start(bf16[4,1,256,128]{3,2,1,0:T(8,128)(2,1)} %broadcast_in_dim.23), calls=%async_computation.5 | async-start | bytes 524288 | tf_op jit(solution)/shard_map/all_to_all | solution.py:46
where the time goes:
time: 170 us; the launch traced here: 167 us
  waiting for transfers between devices  66.3 us (39%)
  starting transfers between devices  65.3 us (38%)
  local copies, waits for them, and re-layouts  18.2 us (11%)
  other arithmetic  9.14 us (5%)
  blocking collectives  3.94 us (2%)
  matrix products  2.97 us (2%)
    all_to_all x4, waiting for transfers between devices, from_everyone(): lax.all_to_all(jnp.broadcast_to(array[None], (count, *array.shape)), axis...  33.3 us
    all_to_all x4, starting transfers between devices, from_everyone(): lax.all_to_all(jnp.broadcast_to(array[None], (count, *array.shape)), axis...  19.6 us
    all_to_all x1, starting transfers between devices, turned_blocks(): lax.all_to_all(tiles, axes[k], split_axis=k, concat_axis=k, tiled=True)  12.7 us
    all_to_all x1, waiting for transfers between devices, shards(): lax.all_to_all(leaving, LOOP, split_axis=0, concat_axis=1, tiled=True)  10.1 us
    all_to_all x1, waiting for transfers between devices, shards(): lax.all_to_all(grad_recv, LOOP, split_axis=0, concat_axis=1, tiled=True)  8.8 us
    ppermute x4, starting transfers between devices, from_partner(): return lax.ppermute(value, axis, pairs)  8.58 us
    all_to_all x1, starting transfers between devices, shards(): lax.all_to_all(grad_recv, LOOP, split_axis=0, concat_axis=1, tiled=True)  8.41 us
    all_to_all x1, starting transfers between devices, shards(): lax.all_to_all(leaving, LOOP, split_axis=0, concat_axis=1, tiled=True)  8.16 us
  transfers between devices with their start and end apart: 12, of which 8 were waited for; matrix products, arithmetic and copies ran while one was open for 12% of the time, Pallas kernels for 0%

commit v1 on v0

v1 whole, which is shorter than its diff:
```python
import functools
import math

import jax
import jax.numpy as jnp
from jax import lax
from jax.experimental import pallas as pl
from jax.experimental.pallas import tpu as pltpu
from jax.sharding import PartitionSpec as P

MESH = pl.DeviceIdType.MESH
WIDE = jnp.float32
NARROW = jnp.bfloat16
NX = 4
NY = 8
NZC = 4
N = NX * NY * NZC


def dot(a, b, ca, cb):
    return lax.dot_general(a, b, (((ca,), (cb,)), ((), ())), preferred_element_type=WIDE)


def gelu_parts(pre_act):
    cumul = 0.5 * (1.0 + lax.erf(pre_act * (1.0 / math.sqrt(2.0))))
    slope = cumul + pre_act * jnp.exp(-0.5 * pre_act * pre_act) * (1.0 / math.sqrt(2.0 * math.pi))
    return (pre_act * cumul, slope)


def exchange(
    x_ref, d_ref, uf_ref, us_ref, df_ref, ds_ref, pu_ref, pd_ref,
    mixed_ref, gtok_ref, grads_ref,
    xb, db, sent, got, act, slope, halves, halves_out, halves_in, part, pieces, total, every,
    near_sem, far_sem, pair_send, pair_recv, send_sem, recv_sem, half_send, half_recv,
    scat_send, scat_recv, gath_send, gath_recv,
):
    me = lax.axis_index("loop")
    dp = lax.axis_index("dp")
    n_dp = lax.axis_size("dp")
    core = lax.rem(me, 2)
    zc = lax.rem(me, NZC)
    z = lax.div(zc, 2)
    y = lax.rem(lax.div(me, NZC), NY)
    x = lax.div(me, NZC * NY)
    half = x_ref.shape[0]
    tok = x_ref.shape[1]
    rows = 2 * N

    def moved(dx, dy, dz, dc):
        return (
            (lax.rem(x + dx, NX) * NY + lax.rem(y + dy, NY)) * NZC
            + lax.rem(z + dz, 2) * 2
            + lax.rem(core + dc, 2)
        )

    partner = moved(0, 0, 0, 1)
    along_y = [moved(0, k, 0, 0) for k in range(1, NY)]
    along_x = [moved(k, 0, 0, 0) for k in range(1, NX)]
    along_z = [moved(0, 0, 0, 1), moved(0, 0, 1, 0), moved(0, 0, 1, 1)]

    def signal(sem, who, group):
        pl.semaphore_signal(sem, 1, device_id=(group, who), device_id_type=MESH)

    barrier = pltpu.get_barrier_semaphore()
    for who in along_y + along_x + along_z:
        signal(barrier, who, dp)
    for k in range(1, n_dp):
        signal(barrier, me, lax.rem(dp + k, n_dp))

    down = lax.broadcasted_iota(jnp.int32, (N, N), 0)
    row_up = (down == pu_ref[...]).astype(NARROW)
    row_down = (down == pd_ref[...]).astype(NARROW)
    lane = lax.broadcasted_iota(jnp.int32, (N, rows), 1)
    sub = lax.broadcasted_iota(jnp.int32, (N, rows), 0)
    spread = [(lane == 2 * sub + b).astype(NARROW) for b in range(2)]
    pick_up = [dot(row_up, e, 0, 0).astype(NARROW) for e in spread]
    pick_down = [dot(row_down, e, 1, 0).astype(NARROW) for e in spread]
    w_up = jnp.concatenate([dot(us_ref[b], pick_up[b], 1, 0).astype(NARROW) for b in range(2)], 0)
    w_down = jnp.concatenate(
        [dot(pick_down[b], df_ref[b], 0, 0).astype(NARROW) for b in range(2)], 1
    )

    xb[core] = x_ref[...]
    db[core] = d_ref[...]
    pl.semaphore_wait(barrier, NY - 1 + NX - 1 + 3 + n_dp - 1)

    to_pair = []
    for i, (src, dst) in enumerate(((x_ref, xb), (d_ref, db))):
        copy = pltpu.make_async_remote_copy(
            src, dst.at[core], pair_send.at[i], pair_recv.at[i],
            device_id=(dp, partner), device_id_type=MESH,
        )
        copy.start()
        to_pair.append(copy)
    for who in along_x:
        signal(near_sem, who, dp)

    def send(i, first, last):
        def one(k, carry):
            dzc = lax.div(k, NX * NY)
            rest = lax.rem(k, NX * NY)
            who = moved(lax.div(rest, NY), lax.rem(rest, NY), lax.div(dzc, 2), lax.rem(dzc, 2))
            pltpu.make_async_remote_copy(
                sent.at[i, who], got.at[i, me], send_sem.at[i], recv_sem.at[i],
                device_id=(dp, who), device_id_type=MESH,
            ).start()
            return carry

        lax.fori_loop(first, last, one, 0)

    def all_of(i, sem):
        return pltpu.make_async_copy(sent.at[i, pl.ds(0, N - 1)], got.at[i, pl.ds(0, N - 1)], sem.at[i])

    def put(i, value):
        sent[i] = value.astype(NARROW).reshape(N, 2, tok)
        got[i, me] = sent[i, me]

    def taken(i):
        all_of(i, recv_sem).wait()
        return got[i].reshape(rows, tok)

    to_pair[0].wait_recv()
    x_block = xb[...].reshape(2 * half, tok)
    put(0, dot(uf_ref[...], x_block, 1, 0))
    pl.semaphore_wait(near_sem, NX - 1)
    for who in along_z:
        signal(far_sem, who, dp)
    send(0, 1, NX * NY)
    to_pair[1].wait_recv()
    d_block = db[...].reshape(2 * half, tok)
    put(1, dot(ds_ref[...], d_block, 1, 0))
    pl.semaphore_wait(far_sem, 3)
    send(0, NX * NY, N)
    send(1, 1, N)

    permuted = taken(0)
    gelu_val, slope_val = gelu_parts(dot(w_up, permuted, 1, 0))
    act[...] = gelu_val.astype(NARROW)
    slope[...] = slope_val
    put(2, dot(w_down, act[...], 1, 0))
    send(2, 1, N)

    grad_rows = taken(1)
    grad_pre = (dot(w_down, grad_rows, 0, 0) * slope[...]).astype(NARROW)
    put(3, dot(w_up, grad_pre, 0, 0))
    send(3, 1, N)

    def chunked(value):
        return value.astype(NARROW).reshape(n_dp, value.shape[0] // n_dp, value.shape[1])

    def scatter(j):
        copies = []
        for k in range(1, n_dp):
            other = lax.rem(dp + k, n_dp)
            copy = pltpu.make_async_remote_copy(
                part.at[j, other], pieces.at[j, k - 1], scat_send.at[j, k - 1],
                scat_recv.at[j, k - 1], device_id=(other, me), device_id_type=MESH,
            )
            copy.start()
            copies.append(copy)
        return copies

    def gather(j, copies):
        value = part[j, dp].astype(WIDE)
        for k in range(1, n_dp):
            copies[k - 1].wait_recv()
            value = value + pieces[j, k - 1].astype(WIDE)
        total[j] = value.astype(NARROW)
        every[j, dp] = total[j]
        out = []
        for k in range(1, n_dp):
            other = lax.rem(dp + k, n_dp)
            copy = pltpu.make_async_remote_copy(
                total.at[j], every.at[j, dp], gath_send.at[j, k - 1],
                gath_recv.at[j, k - 1], device_id=(other, me), device_id_type=MESH,
            )
            copy.start()
            out.append(copy)
        return out

    mixed_up = dot(grad_pre, permuted, 1, 1).astype(NARROW)
    part[1] = chunked(
        jnp.concatenate([dot(mixed_up[N * b : N * b + N], pick_up[b], 1, 1) for b in range(2)], 0)
    )
    scat_up_second = scatter(1)
    mixed_down = dot(grad_rows, act[...], 1, 1).astype(NARROW)
    part[2] = chunked(
        jnp.concatenate([dot(pick_down[b], mixed_down[:, N * b : N * b + N], 1, 0) for b in range(2)], 0)
    )
    scat_down_first = scatter(2)

    def to_partner(i, value):
        halves[i] = value.reshape(2, half, tok)
        halves_out[i] = halves[i, 1 - core].astype(NARROW)
        copy = pltpu.make_async_remote_copy(
            halves_out.at[i], halves_in.at[i], half_send.at[i], half_recv.at[i],
            device_id=(dp, partner), device_id_type=MESH,
        )
        copy.start()
        return copy

    back_rows = taken(2)
    part[3] = chunked(dot(back_rows, d_block, 1, 1))
    scat_down_second = scatter(3)
    out_half = to_partner(0, dot(ds_ref[...], back_rows, 0, 0))
    gath_up_second = gather(1, scat_up_second)
    gath_down_first = gather(2, scat_down_first)

    grad_hidden = taken(3)
    part[0] = chunked(dot(grad_hidden, x_block, 1, 1))
    scat_up_first = scatter(0)
    grad_half = to_partner(1, dot(uf_ref[...], grad_hidden, 0, 0))
    gath_down_second = gather(3, scat_down_second)

    out_half.wait_recv()
    mixed_ref[...] = (
        x_ref[...].astype(WIDE) + (halves[0, core] + halves_in[0].astype(WIDE))
    ).astype(NARROW)
    grad_half.wait_recv()
    gtok_ref[...] = (
        d_ref[...].astype(WIDE) + (halves[1, core] + halves_in[1].astype(WIDE))
    ).astype(NARROW)
    gath_up_first = gather(0, scat_up_first)

    for j, copies in ((1, gath_up_second), (2, gath_down_first), (3, gath_down_second), (0, gath_up_first)):
        for copy in copies:
            copy.wait_recv()
        grads_ref[j] = every[j].reshape(rows, N)

    for copy in to_pair + [out_half, grad_half]:
        copy.wait_send()
    for copies in (
        scat_up_second, scat_down_first, scat_down_second, scat_up_first,
        gath_up_second, gath_down_first, gath_down_second, gath_up_first,
    ):
        for copy in copies:
            copy.wait_send()
    for i in range(4):
        all_of(i, send_sem).wait()


def finish(scale, mixed_in, gtok_in, grads_in, mixed_ref, gtok_ref, uf_ref, us_ref, df_ref, ds_ref):
    mixed_ref[...] = mixed_in[...]
    gtok_ref[...] = gtok_in[...]
    for j, ref in enumerate((uf_ref, us_ref, df_ref, ds_ref)):
        ref[...] = (grads_in[j].astype(WIDE) * scale).reshape(ref.shape)


def shards(tokens, cotangent, up_first, up_second, down_first, down_second, perm_up, perm_down):
    half, tok = tokens.shape
    block = up_first.shape[2]
    rows = 2 * N
    n_dp = lax.axis_size("dp")
    vmem = pl.BlockSpec(memory_space=pltpu.VMEM)
    regular = pltpu.SemaphoreType.REGULAR
    dma = pltpu.SemaphoreType.DMA
    small = jax.ShapeDtypeStruct((half, tok), NARROW)
    mixed, gtok, grads = pl.pallas_call(
        exchange,
        name="exchange",
        out_shape=(small, small, jax.ShapeDtypeStruct((4, rows, block), NARROW)),
        in_specs=[vmem] * 8,
        out_specs=(vmem,) * 3,
        scratch_shapes=[
            pltpu.VMEM((2, half, tok), NARROW),
            pltpu.VMEM((2, half, tok), NARROW),
            pltpu.VMEM((4, N, 2, tok), NARROW),
            pltpu.VMEM((4, N, 2, tok), NARROW),
            pltpu.VMEM((rows, tok), NARROW),
            pltpu.VMEM((rows, tok), WIDE),
            pltpu.VMEM((2, 2, half, tok), WIDE),
            pltpu.VMEM((2, half, tok), NARROW),
            pltpu.VMEM((2, half, tok), NARROW),
            pltpu.VMEM((4, n_dp, rows // n_dp, block), NARROW),
            pltpu.VMEM((4, n_dp - 1, rows // n_dp, block), NARROW),
            pltpu.VMEM((4, rows // n_dp, block), NARROW),
            pltpu.VMEM((4, n_dp, rows // n_dp, block), NARROW),
            regular,
            regular,
            dma((2,)),
            dma((2,)),
            dma((4,)),
            dma((4,)),
            dma((2,)),
            dma((2,)),
            dma((4, n_dp - 1)),
            dma((4, n_dp - 1)),
            dma((4, n_dp - 1)),
            dma((4, n_dp - 1)),
        ],
        compiler_params=pltpu.CompilerParams(collective_id=0, has_side_effects=True),
    )(
        tokens, cotangent, up_first.reshape(rows, block), up_second, down_first,
        down_second.reshape(rows, block), perm_up.reshape(1, N), perm_down.reshape(1, N),
    )
    scale = 1.0 / math.sqrt(n_dp * tok)
    first = jax.ShapeDtypeStruct((1, rows, block), WIDE)
    second = jax.ShapeDtypeStruct((2, block, block), WIDE)
    return pl.pallas_call(
        functools.partial(finish, scale),
        name="finish",
        out_shape=(small, small, first, second, second, first),
        in_specs=[vmem] * 3,
        out_specs=(vmem,) * 6,
    )(mixed, gtok, grads)


def solution(mesh):
    spread = P("loop", "dp")
    weight = P("loop", None, None)
    return jax.shard_map(
        shards,
        mesh=mesh,
        in_specs=(spread, spread, weight, weight, weight, weight, P(), P()),
        out_specs=(spread, spread, weight, weight, weight, weight),
        check_vma=False,
    )
```

time: 170 us -> 62.1 us (0.37); the launches traced: 167 us -> 61.9 us
  waiting for transfers between devices: 66.3 us -> 0 us
  starting transfers between devices: 65.3 us -> 0 us
  Pallas kernels: 0 us -> 61.3 us
  local copies, waits for them, and re-layouts: 18.2 us -> 0 us
  other arithmetic: 9.14 us -> 0 us
  blocking collectives: 3.94 us -> 0 us
  matrix products: 2.97 us -> 0 us
    all_to_all x8 -> x0, waiting for transfers between devices: 66.3 us -> none  [the longest x4 33.3 us: from_everyone(): lax.all_to_all(jnp.broadcast_to(array[None], (count, *array.shape)), axis...]
    pallas_call x0 -> x2, Pallas kernels: none -> 61.3 us  [the longest x1 59.4 us: shards(): pl.pallas_call(exchange, name='exchange', out_shape=(small, small, jax.Sh...]
    all_to_all x8 -> x0, starting transfers between devices: 56.8 us -> none  [the longest x4 19.6 us: from_everyone(): lax.all_to_all(jnp.broadcast_to(array[None], (count, *array.shape)), axis...]
    ppermute x4 -> x0, starting transfers between devices: 8.58 us -> none  [from_partner(): return lax.ppermute(value, axis, pairs)]
    unnamed x19 -> x0, local copies, waits for them, and re-layouts: 4.93 us -> none
    gather x4 -> x0, local copies, waits for them, and re-layouts: 4.51 us -> none  [the longest x1 1.13 us: shards(): jnp.take(core_and_chips(hidden_one, (('loop_0', 'loop_1', 'loop_2'), 'loo...]
    all_to_all x1 -> x0, blocking collectives: 3.94 us -> none  [turned_blocks(): lax.all_to_all(tiles, axes[k], split_axis=k, concat_axis=k, tiled=True)]
    dot_general x12 -> x0, matrix products: 2.97 us -> none  [the longest x1 0.36 us: shards(): jnp.einsum('bpo,pbt->bot', down_first, grad_mixed, preferred_element_type...]
  transfers between devices with their start and end apart: 12 -> 0, of which waited for: 8 -> 0; matrix products, arithmetic and copies ran while one was open for 12% -> 0% of each run, Pallas kernels for 0% -> 0%
where the time goes in v1:
time: 62.1 us; the launch traced here: 61.9 us
  Pallas kernels  61.3 us (99%)
  between operations  0.64 us (1%)
    pallas_call x1, Pallas kernels, shards(): pl.pallas_call(exchange, name='exchange', out_shape=(small, small, jax.Sh...  59.4 us
    pallas_call x1, Pallas kernels, shards(): pl.pallas_call(functools.partial(finish, scale), name='finish', out_shape...  1.86 us

profile of v1, /device:TPU:6, one launch (start us, length us, event | category | flops | bytes accessed | tf_op | source)
XLA Modules:
  0.0 61.9 jit_solution(17028606045903896715)
XLA Ops:
  0.6 59.4 %exchange.1 = (bf16[64,512]{1,0:T(8,128)(2,1)}, bf16[64,512]{1,0:T(8,128)(2,1)}, bf16[4,256,128]{2,1,0:T(8,128)(2,1)}) custom-call(bf16[64,512]{1,0:T(8,128)(2,1)} %x_ref.1, bf16[64,512]{1,0:T(8,128)(2,1)} %d_ref.1, bf16[256,128]{1,0:T(8,128)(2,1)} %bitcast.4, bf16[2,128,128]{2,1,0:T(8,128)(2,1)} %us_ref.1, bf16[2,128,128]{2,1,0:T(8,128)(2,1)} %df_ref.1, ...), custom_call_target="tpu_custom_call" | custom-call | tf_op jit(solution)/shard_map/exchange/pallas_call | solution.py:258
  60.1 1.9 %finish.1 = (bf16[64,512]{1,0:T(8,128)(2,1)}, bf16[64,512]{1,0:T(8,128)(2,1)}, f32[1,256,128]{2,1,0:T(8,128)}, f32[2,128,128]{2,1,0:T(8,128)}, f32[2,128,128]{2,1,0:T(8,128)}, /*index=5*/f32[1,256,128]{2,1,0:T(8,128)}) custom-call(bf16[64,512]{1,0:T(8,128)(2,1)} %get-tuple-element.9.mixed_in, bf16[64,512]{1,0:T(8,128)(2,1)} %get-tuple-element.10.gtok_in, ...), custom_call_target="tpu_custom_call" | custom-call | tf_op jit(solution)/shard_map/finish/pallas_call | solution.py:299

commit v2 on v1

v2 whole, which is shorter than its diff:
```python
import functools
import math

import jax
import jax.numpy as jnp
from jax import lax
from jax.experimental import pallas as pl
from jax.experimental.pallas import tpu as pltpu
from jax.sharding import PartitionSpec as P

MESH = pl.DeviceIdType.MESH
WIDE = jnp.float32
NARROW = jnp.bfloat16
NX = 4
NY = 8
NZC = 4
N = NX * NY * NZC
DIRECT = (2, 3)


def dot(a, b, ca, cb):
    return lax.dot_general(a, b, (((ca,), (cb,)), ((), ())), preferred_element_type=WIDE)


def gelu_parts(pre_act):
    cumul = 0.5 * (1.0 + lax.erf(pre_act * (1.0 / math.sqrt(2.0))))
    slope = cumul + pre_act * jnp.exp(-0.5 * pre_act * pre_act) * (1.0 / math.sqrt(2.0 * math.pi))
    return (pre_act * cumul, slope)


def exchange(
    x_hbm, d_hbm, uf_hbm, us_hbm, df_hbm, ds_hbm, pu_hbm, pd_hbm,
    mixed_ref, gtok_ref, grads_ref,
    xb, db, uf_ref, us_ref, df_ref, ds_ref, pu_ref, pd_ref,
    sent, got, act, slope, halves, halves_out, halves_in,
    part, pieces, total, every, qpart, qpieces, qtotal, qevery, whole, wholes,
    near_sem, far_sem, load_sem, pair_send, pair_recv, send_sem, recv_sem, half_send, half_recv,
    scat_send, scat_recv, gath_send, gath_recv, qscat_send, qscat_recv, qgath_send, qgath_recv,
):
    me = lax.axis_index("loop")
    dp = lax.axis_index("dp")
    n_dp = lax.axis_size("dp")
    core = lax.rem(me, 2)
    zc = lax.rem(me, NZC)
    z = lax.div(zc, 2)
    y = lax.rem(lax.div(me, NZC), NY)
    x = lax.div(me, NZC * NY)
    plane = NY * NZC
    half = xb.shape[1]
    tok = xb.shape[2]
    rows = 2 * N

    def moved(dx, dy, dz, dc):
        return (
            (lax.rem(x + dx, NX) * NY + lax.rem(y + dy, NY)) * NZC
            + lax.rem(z + dz, 2) * 2
            + lax.rem(core + dc, 2)
        )

    partner = moved(0, 0, 0, 1)
    along_y = [moved(0, k, 0, 0) for k in range(1, NY)]
    along_x = [moved(k, 0, 0, 0) for k in range(1, NX)]
    along_z = [moved(0, 0, 0, 1), moved(0, 0, 1, 0), moved(0, 0, 1, 1)]

    def signal(sem, who, group):
        pl.semaphore_signal(sem, 1, device_id=(group, who), device_id_type=MESH)

    barrier = pltpu.get_barrier_semaphore()
    for who in along_y + along_x + along_z:
        signal(barrier, who, dp)
    for k in range(1, n_dp):
        signal(barrier, me, lax.rem(dp + k, n_dp))

    loads = []
    for i, (src, dst) in enumerate(
        (
            (x_hbm, xb.at[core]), (d_hbm, db.at[core]), (uf_hbm, uf_ref), (ds_hbm, ds_ref),
            (us_hbm, us_ref), (df_hbm, df_ref), (pu_hbm, pu_ref), (pd_hbm, pd_ref),
        )
    ):
        copy = pltpu.make_async_copy(src, dst, load_sem.at[i])
        copy.start()
        loads.append(copy)

    def remote(src, dst, send, recv, group, who):
        copy = pltpu.make_async_remote_copy(
            src, dst, send, recv, device_id=(group, who), device_id_type=MESH
        )
        copy.start()
        return copy

    pl.semaphore_wait(barrier, NY - 1 + NX - 1 + 3 + n_dp - 1)
    for who in along_x:
        signal(near_sem, who, dp)
    to_pair = [
        remote(src, dst.at[core], pair_send.at[i], pair_recv.at[i], dp, partner)
        for i, (src, dst) in enumerate(((x_hbm, xb), (d_hbm, db)))
    ]
    pl.semaphore_wait(near_sem, NX - 1)
    for who in along_z:
        signal(far_sem, who, dp)

    def send(i, first, last):
        def one(k, carry):
            dzc = lax.div(k, NX * NY)
            rest = lax.rem(k, NX * NY)
            who = moved(lax.div(rest, NY), lax.rem(rest, NY), lax.div(dzc, 2), lax.rem(dzc, 2))
            remote(sent.at[i, who], got.at[i, me], send_sem.at[i], recv_sem.at[i, 0], dp, who)
            return carry

        lax.fori_loop(first, last, one, 0)

    def send_planes(i):
        for dx in range(NX):

            def one(k, carry, dx=dx):
                dzc = lax.div(k, NY)
                who = moved(dx, lax.rem(k, NY), lax.div(dzc, 2), lax.rem(dzc, 2))
                remote(sent.at[i, who], got.at[i, me], send_sem.at[i], recv_sem.at[i, dx], dp, who)
                return carry

            lax.fori_loop(0 if dx else 1, plane, one, 0)

    def landed(i, count, sem):
        return pltpu.make_async_copy(sent.at[i, pl.ds(0, count)], got.at[i, pl.ds(0, count)], sem)

    def put(i, value):
        sent[i] = value.astype(NARROW).reshape(N, 2, tok)
        got[i, me] = sent[i, me]

    def taken(i):
        landed(i, N - 1, recv_sem.at[i, 0]).wait()
        return got[i].reshape(rows, tok)

    loads[0].wait()
    loads[2].wait()
    to_pair[0].wait_recv()
    x_block = xb[...].reshape(2 * half, tok)
    put(0, dot(uf_ref[...], x_block, 1, 0))
    send(0, 1, NX * NY)
    loads[1].wait()
    loads[3].wait()
    to_pair[1].wait_recv()
    d_block = db[...].reshape(2 * half, tok)
    put(1, dot(ds_ref[...], d_block, 1, 0))
    pl.semaphore_wait(far_sem, 3)
    send(0, NX * NY, N)
    send(1, 1, N)

    for copy in loads[4:]:
        copy.wait()
    down = lax.broadcasted_iota(jnp.int32, (N, N), 0)
    row_up = (down == pu_ref[...]).astype(NARROW)
    row_down = (down == pd_ref[...]).astype(NARROW)
    lane = lax.broadcasted_iota(jnp.int32, (N, rows), 1)
    sub = lax.broadcasted_iota(jnp.int32, (N, rows), 0)
    spread = [(lane == 2 * sub + b).astype(NARROW) for b in range(2)]
    pick_up = [dot(row_up, e, 0, 0).astype(NARROW) for e in spread]
    pick_down = [dot(row_down, e, 1, 0).astype(NARROW) for e in spread]
    w_up = jnp.concatenate([dot(us_ref[b], pick_up[b], 1, 0).astype(NARROW) for b in range(2)], 0)
    w_down = jnp.concatenate(
        [dot(pick_down[b], df_ref[b], 0, 0).astype(NARROW) for b in range(2)], 1
    )

    permuted = taken(0)
    gelu_val, slope_val = gelu_parts(dot(w_up, permuted, 1, 0))
    act[...] = gelu_val.astype(NARROW)
    slope[...] = slope_val
    put(2, dot(w_down, act[...], 1, 0))
    send_planes(2)

    grad_rows = taken(1)
    grad_pre = (dot(w_down, grad_rows, 0, 0) * slope[...]).astype(NARROW)
    put(3, dot(w_up, grad_pre, 0, 0))
    send_planes(3)

    others = [lax.rem(dp + k, n_dp) for k in range(1, n_dp)]
    sends = list(to_pair)

    def spread_out(own, slots, send_at, recv_at):
        copies = [
            remote(own(other), slots(k), send_at.at[k], recv_at.at[k], other, me)
            for k, other in enumerate(others)
        ]
        sends.extend(copies)
        return copies

    def scatter(src, dst, send_at, recv_at):
        return spread_out(lambda other: src.at[other], lambda k: dst.at[k], send_at, recv_at)

    def gather(copies, src, landing, sums, dst, send_at, recv_at):
        value = src[dp].astype(WIDE)
        for k, copy in enumerate(copies):
            copy.wait_recv()
            value = value + landing[k].astype(WIDE)
        sums[...] = value.astype(NARROW)
        dst[dp] = sums[...]
        return spread_out(lambda other: sums, lambda k: dst.at[dp], send_at, recv_at)

    def chunked(value):
        return value.astype(NARROW).reshape(n_dp, value.shape[0] // n_dp, value.shape[1])

    def scatter_block(j):
        return scatter(part.at[j], pieces.at[j], scat_send.at[j], scat_recv.at[j])

    def gather_block(j, copies):
        return gather(
            copies, part.at[j], pieces.at[j], total.at[j], every.at[j], gath_send.at[j], gath_recv.at[j]
        )

    def scatter_plane(s, q):
        return scatter(qpart.at[s, q], qpieces.at[s, q], qscat_send.at[s, q], qscat_recv.at[s, q])

    def gather_plane(s, q, copies):
        return gather(
            copies, qpart.at[s, q], qpieces.at[s, q], qtotal.at[s, q], qevery.at[s, q],
            qgath_send.at[s, q], qgath_recv.at[s, q],
        )

    def plane_of(q):
        return lax.rem(x + NX - q, NX)

    def plane_rows(i, q):
        landed(i, plane if q else plane - 1, recv_sem.at[i, q]).wait()
        return got[i, pl.ds(plane_of(q) * plane, plane)].reshape(2 * plane, tok)

    mixed_up = dot(grad_pre, permuted, 1, 1).astype(NARROW)
    part[0] = chunked(
        jnp.concatenate([dot(mixed_up[N * b : N * b + N], pick_up[b], 1, 1) for b in range(2)], 0)
    )
    scat_up = scatter_block(0)
    mixed_down = dot(grad_rows, act[...], 1, 1).astype(NARROW)
    part[1] = chunked(
        jnp.concatenate([dot(pick_down[b], mixed_down[:, N * b : N * b + N], 1, 0) for b in range(2)], 0)
    )
    scat_down = scatter_block(1)

    def to_partner(i, value):
        halves[i] = value.reshape(2, half, tok)
        halves_out[i] = halves[i, 1 - core].astype(NARROW)
        copy = remote(halves_out.at[i], halves_in.at[i], half_send.at[i], half_recv.at[i], dp, partner)
        sends.append(copy)
        return copy

    def joined(i, base, copy):
        copy.wait_recv()
        return (
            base[core].astype(WIDE) + (halves[i, core] + halves_in[i].astype(WIDE))
        ).astype(NARROW)

    def plane_grad(s, q, block):
        value = dot(plane_rows(2 + s, q), block, 1, 1)
        if s == 1 and q in DIRECT:
            whole[q] = value.astype(NARROW)
            wholes[q, dp] = whole[q]
            return spread_out(
                lambda other: whole.at[q], lambda k: wholes.at[q, dp], qscat_send.at[s, q],
                qscat_recv.at[s, q],
            )
        qpart[s, q] = chunked(value)
        return scatter_plane(s, q)

    scat_second = [plane_grad(0, q, d_block) for q in range(NX)]
    out_half = to_partner(0, dot(ds_ref[...], got[2].reshape(rows, tok), 0, 0))
    gath_up = gather_block(0, scat_up)
    gath_down = gather_block(1, scat_down)
    scat_first = [plane_grad(1, 0, x_block), plane_grad(1, 1, x_block)]
    gath_second = [gather_plane(0, q, scat_second[q]) for q in range(NX)]
    scat_first += [plane_grad(1, q, x_block) for q in range(2, NX)]
    grad_half = to_partner(1, dot(uf_ref[...], got[3].reshape(rows, tok), 0, 0))
    mixed_ref[...] = joined(0, xb, out_half)
    gath_first = [None if q in DIRECT else gather_plane(1, q, scat_first[q]) for q in range(NX)]
    gtok_ref[...] = joined(1, db, grad_half)

    for j, copies in ((0, gath_up), (1, gath_down)):
        for copy in copies:
            copy.wait_recv()
        grads_ref[1 + j] = every[j].reshape(NX, 2 * plane, N)
    for s, j, found in ((0, 3, gath_second), (1, 0, gath_first)):
        for q in range(NX):
            for copy in found[q] or scat_first[q]:
                copy.wait_recv()
            if found[q]:
                grads_ref[j, plane_of(q)] = qevery[s, q].reshape(2 * plane, N)
            else:
                value = wholes[q, 0].astype(WIDE)
                for k in range(1, n_dp):
                    value = value + wholes[q, k].astype(WIDE)
                grads_ref[j, plane_of(q)] = value.astype(NARROW)

    for copy in sends:
        copy.wait_send()
    for i in range(4):
        landed(i, N - 1, send_sem.at[i]).wait()


def finish(scale, mixed_in, gtok_in, grads_in, mixed_ref, gtok_ref, uf_ref, us_ref, df_ref, ds_ref):
    mixed_ref[...] = mixed_in[...]
    gtok_ref[...] = gtok_in[...]
    for j, ref in enumerate((uf_ref, us_ref, df_ref, ds_ref)):
        ref[...] = (grads_in[j].astype(WIDE) * scale).reshape(ref.shape)


def shards(tokens, cotangent, up_first, up_second, down_first, down_second, perm_up, perm_down):
    half, tok = tokens.shape
    block = up_first.shape[2]
    rows = 2 * N
    n_dp = lax.axis_size("dp")
    vmem = pl.BlockSpec(memory_space=pltpu.VMEM)
    regular = pltpu.SemaphoreType.REGULAR
    dma = pltpu.SemaphoreType.DMA
    small = jax.ShapeDtypeStruct((half, tok), NARROW)
    some = rows // n_dp
    few = some // NX
    mixed, gtok, grads = pl.pallas_call(
        exchange,
        name="exchange",
        out_shape=(
            pltpu.VMEM((half, tok), NARROW),
            pltpu.VMEM((half, tok), NARROW),
            pltpu.VMEM((4, NX, rows // NX, block), NARROW),
        ),
        in_specs=[pl.BlockSpec(memory_space=pl.ANY)] * 8,
        out_specs=(vmem,) * 3,
        scratch_shapes=[
            pltpu.VMEM((2, half, tok), NARROW),
            pltpu.VMEM((2, half, tok), NARROW),
            pltpu.VMEM((rows, block), NARROW),
            pltpu.VMEM((2, block, block), NARROW),
            pltpu.VMEM((2, block, block), NARROW),
            pltpu.VMEM((rows, block), NARROW),
            pltpu.VMEM((1, N), jnp.int32),
            pltpu.VMEM((1, N), jnp.int32),
            pltpu.VMEM((4, N, 2, tok), NARROW),
            pltpu.VMEM((4, N, 2, tok), NARROW),
            pltpu.VMEM((rows, tok), NARROW),
            pltpu.VMEM((rows, tok), WIDE),
            pltpu.VMEM((2, 2, half, tok), WIDE),
            pltpu.VMEM((2, half, tok), NARROW),
            pltpu.VMEM((2, half, tok), NARROW),
            pltpu.VMEM((2, n_dp, some, block), NARROW),
            pltpu.VMEM((2, n_dp - 1, some, block), NARROW),
            pltpu.VMEM((2, some, block), NARROW),
            pltpu.VMEM((2, n_dp, some, block), NARROW),
            pltpu.VMEM((2, NX, n_dp, few, block), NARROW),
            pltpu.VMEM((2, NX, n_dp - 1, few, block), NARROW),
            pltpu.VMEM((2, NX, few, block), NARROW),
            pltpu.VMEM((2, NX, n_dp, few, block), NARROW),
            pltpu.VMEM((NX, rows // NX, block), NARROW),
            pltpu.VMEM((NX, n_dp, rows // NX, block), NARROW),
            regular,
            regular,
            dma((8,)),
            dma((2,)),
            dma((2,)),
            dma((4,)),
            dma((4, NX)),
            dma((2,)),
            dma((2,)),
            *(dma((2, n_dp - 1)),) * 4,
            *(dma((2, NX, n_dp - 1)),) * 4,
        ],
        compiler_params=pltpu.CompilerParams(collective_id=0, has_side_effects=True),
    )(
        tokens, cotangent, up_first.reshape(rows, block), up_second, down_first,
        down_second.reshape(rows, block), perm_up.reshape(1, N), perm_down.reshape(1, N),
    )
    scale = 1.0 / math.sqrt(n_dp * tok)
    first = jax.ShapeDtypeStruct((1, rows, block), WIDE)
    second = jax.ShapeDtypeStruct((2, block, block), WIDE)
    return pl.pallas_call(
        functools.partial(finish, scale),
        name="finish",
        out_shape=(small, small, first, second, second, first),
        in_specs=[vmem] * 3,
        out_specs=(vmem,) * 6,
    )(*(pltpu.with_memory_space_constraint(v, pltpu.VMEM) for v in (mixed, gtok, grads)))


def solution(mesh):
    spread = P("loop", "dp")
    weight = P("loop", None, None)
    return jax.shard_map(
        shards,
        mesh=mesh,
        in_specs=(spread, spread, weight, weight, weight, weight, P(), P()),
        out_specs=(spread, spread, weight, weight, weight, weight),
        check_vma=False,
    )
```

time: 62.1 us -> 59.6 us (0.960)
  Pallas kernels: 61.3 us -> 58.8 us
    pallas_call x1, Pallas kernels: 59.4 us -> 57.9 us  [shards(): pl.pallas_call(exchange, name='exchange', out_shape=(pltpu.VMEM((half, to...]
    pallas_call x1, Pallas kernels: 1.86 us -> 0.87 us  [shards(): pl.pallas_call(functools.partial(finish, scale), name='finish', out_shape...]
where the time goes in v2:
time: 59.6 us; the launch traced here: 59.5 us
  Pallas kernels  58.8 us (99%)
  between operations  0.64 us (1%)
    pallas_call x1, Pallas kernels, shards(): pl.pallas_call(exchange, name='exchange', out_shape=(pltpu.VMEM((half, to...  57.9 us

profile of v2, /device:TPU:6, one launch (start us, length us, event | category | flops | bytes accessed | tf_op | source)
XLA Modules:
  0.0 59.5 jit_solution(1434323572807033076)
XLA Ops:
  0.6 57.9 %exchange.1 = (bf16[64,512]{1,0:T(8,128)(2,1)S(1)}, bf16[64,512]{1,0:T(8,128)(2,1)S(1)}, bf16[4,4,64,128]{3,2,1,0:T(8,128)(2,1)S(1)}) custom-call(bf16[64,512]{1,0:T(8,128)(2,1)} %x_hbm.1, bf16[64,512]{1,0:T(8,128)(2,1)} %d_hbm.1, bf16[256,128]{1,0:T(8,128)(2,1)} %bitcast.4, bf16[2,128,128]{2,1,0:T(8,128)(2,1)} %us_hbm.1, bf16[2,128,128]{2,1,0:T(8,128)(2,1)} %df_hbm.1, ...), custom_call_target="tpu_custom_call" | custom-call | tf_op jit(solution)/shard_map/exchange/pallas_call | solution.py:315
  58.6 0.9 %finish.1 = (bf16[64,512]{1,0:T(8,128)(2,1)}, bf16[64,512]{1,0:T(8,128)(2,1)}, f32[1,256,128]{2,1,0:T(8,128)}, f32[2,128,128]{2,1,0:T(8,128)}, f32[2,128,128]{2,1,0:T(8,128)}, /*index=5*/f32[1,256,128]{2,1,0:T(8,128)}) custom-call(bf16[64,512]{1,0:T(8,128)(2,1)S(1)} %get-tuple-element.9.mixed_in, bf16[64,512]{1,0:T(8,128)(2,1)S(1)} %get-tuple-element.10.gtok_in, ...), custom_call_target="tpu_custom_call" | custom-call | tf_op jit(solution)/shard_map/finish/pallas_call | solution.py:371

commit v3 on v2

--- a/solution.py
+++ b/solution.py
@@ -34,7 +34,7 @@
     xb, db, uf_ref, us_ref, df_ref, ds_ref, pu_ref, pd_ref,
     sent, got, act, slope, halves, halves_out, halves_in,
     part, pieces, total, every, qpart, qpieces, qtotal, qevery, whole, wholes,
-    near_sem, far_sem, load_sem, pair_send, pair_recv, send_sem, recv_sem, half_send, half_recv,
+    near_sem, far_sem, shard_sem, load_sem, pair_send, pair_recv, send_sem, recv_sem, half_send, half_recv,
     scat_send, scat_recv, gath_send, gath_recv, qscat_send, qscat_recv, qgath_send, qgath_recv,
 ):
     me = lax.axis_index("loop")
@@ -69,7 +69,10 @@
     for who in along_y + along_x + along_z:
         signal(barrier, who, dp)
     for k in range(1, n_dp):
-        signal(barrier, me, lax.rem(dp + k, n_dp))
+
+        @pl.when(dp + k < n_dp)
+        def _(k=k):
+            signal(barrier, me, dp + k)
 
     loads = []
     for i, (src, dst) in enumerate(
@@ -89,34 +92,32 @@
         copy.start()
         return copy
 
-    pl.semaphore_wait(barrier, NY - 1 + NX - 1 + 3 + n_dp - 1)
-    for who in along_x:
+    pl.semaphore_wait(barrier, NY - 1 + NX - 1 + 3 + dp)
+    for who in along_z:
         signal(near_sem, who, dp)
     to_pair = [
         remote(src, dst.at[core], pair_send.at[i], pair_recv.at[i], dp, partner)
         for i, (src, dst) in enumerate(((x_hbm, xb), (d_hbm, db)))
     ]
-    pl.semaphore_wait(near_sem, NX - 1)
-    for who in along_z:
+    pl.semaphore_wait(near_sem, 3)
+    for who in along_x:
         signal(far_sem, who, dp)
-
-    def send(i, first, last):
-        def one(k, carry):
-            dzc = lax.div(k, NX * NY)
-            rest = lax.rem(k, NX * NY)
-            who = moved(lax.div(rest, NY), lax.rem(rest, NY), lax.div(dzc, 2), lax.rem(dzc, 2))
-            remote(sent.at[i, who], got.at[i, me], send_sem.at[i], recv_sem.at[i, 0], dp, who)
-            return carry
-
-        lax.fori_loop(first, last, one, 0)
-
-    def send_planes(i):
-        for dx in range(NX):
-
-            def one(k, carry, dx=dx):
-                dzc = lax.div(k, NY)
-                who = moved(dx, lax.rem(k, NY), lax.div(dzc, 2), lax.rem(dzc, 2))
-                remote(sent.at[i, who], got.at[i, me], send_sem.at[i], recv_sem.at[i, dx], dp, who)
+    for k in range(1, n_dp):
+
+        @pl.when(dp >= k)
+        def _(k=k):
+            signal(shard_sem, me, dp - k)
+
+    spot = lax.rem(me, plane)
+
+    def send(i, planes, apart=True):
+        for dx in planes:
+            base = lax.rem(x + dx, NX) * plane
+
+            def one(k, carry, dx=dx, base=base):
+                who = base + lax.rem(spot + k, plane)
+                arrived = recv_sem.at[i, dx if apart else 0]
+                remote(sent.at[i, who], got.at[i, me], send_sem.at[i], arrived, dp, who)
                 return carry
 
             lax.fori_loop(0 if dx else 1, plane, one, 0)
@@ -137,15 +138,15 @@
     to_pair[0].wait_recv()
     x_block = xb[...].reshape(2 * half, tok)
     put(0, dot(uf_ref[...], x_block, 1, 0))
-    send(0, 1, NX * NY)
+    send(0, (0,), False)
     loads[1].wait()
     loads[3].wait()
     to_pair[1].wait_recv()
     d_block = db[...].reshape(2 * half, tok)
     put(1, dot(ds_ref[...], d_block, 1, 0))
-    pl.semaphore_wait(far_sem, 3)
-    send(0, NX * NY, N)
-    send(1, 1, N)
+    pl.semaphore_wait(far_sem, NX - 1)
+    send(0, range(1, NX), False)
+    send(1, range(NX), False)
 
     for copy in loads[4:]:
         copy.wait()
@@ -167,12 +168,17 @@
     act[...] = gelu_val.astype(NARROW)
     slope[...] = slope_val
     put(2, dot(w_down, act[...], 1, 0))
-    send_planes(2)
+    send(2, range(NX))
 
     grad_rows = taken(1)
     grad_pre = (dot(w_down, grad_rows, 0, 0) * slope[...]).astype(NARROW)
     put(3, dot(w_up, grad_pre, 0, 0))
-    send_planes(3)
+    send(3, range(NX))
+
+    @pl.when(dp + 1 < n_dp)
+    def _():
+        pl.semaphore_wait(shard_sem, n_dp - 1 - dp)
+
 
     others = [lax.rem(dp + k, n_dp) for k in range(1, n_dp)]
     sends = list(to_pair)
@@ -350,6 +356,7 @@
             pltpu.VMEM((NX, n_dp, rows // NX, block), NARROW),
             regular,
             regular,
+            regular,
             dma((8,)),
             dma((2,)),
             dma((2,)),

time: 59.6 us -> 56.2 us (0.943)
  Pallas kernels: 58.8 us -> 55.4 us
    pallas_call x1, Pallas kernels: 57.9 us -> 54.5 us  [shards(): pl.pallas_call(exchange, name='exchange', out_shape=(pltpu.VMEM((half, to...]
where the time goes in v3:
time: 56.2 us; the launch traced here: 56 us
  Pallas kernels  55.4 us (99%)
  between operations  0.64 us (1%)
    pallas_call x1, Pallas kernels, shards(): pl.pallas_call(exchange, name='exchange', out_shape=(pltpu.VMEM((half, to...  54.5 us

profile of v3, /device:TPU:6, one launch (start us, length us, event | category | flops | bytes accessed | tf_op | source)
XLA Modules:
  0.0 56.0 jit_solution(2622253723002202344)
XLA Ops:
  0.6 54.5 %exchange.1 = (bf16[64,512]{1,0:T(8,128)(2,1)S(1)}, bf16[64,512]{1,0:T(8,128)(2,1)S(1)}, bf16[4,4,64,128]{3,2,1,0:T(8,128)(2,1)S(1)}) custom-call(bf16[64,512]{1,0:T(8,128)(2,1)} %x_hbm.1, bf16[64,512]{1,0:T(8,128)(2,1)} %d_hbm.1, bf16[256,128]{1,0:T(8,128)(2,1)} %bitcast.4, bf16[2,128,128]{2,1,0:T(8,128)(2,1)} %us_hbm.1, bf16[2,128,128]{2,1,0:T(8,128)(2,1)} %df_hbm.1, ...), custom_call_target="tpu_custom_call" | custom-call | tf_op jit(solution)/shard_map/exchange/pallas_call | solution.py:321
  55.1 0.9 %finish.1 = (bf16[64,512]{1,0:T(8,128)(2,1)}, bf16[64,512]{1,0:T(8,128)(2,1)}, f32[1,256,128]{2,1,0:T(8,128)}, f32[2,128,128]{2,1,0:T(8,128)}, f32[2,128,128]{2,1,0:T(8,128)}, /*index=5*/f32[1,256,128]{2,1,0:T(8,128)}) custom-call(bf16[64,512]{1,0:T(8,128)(2,1)S(1)} %get-tuple-element.9.mixed_in, bf16[64,512]{1,0:T(8,128)(2,1)S(1)} %get-tuple-element.10.gtok_in, ...), custom_call_target="tpu_custom_call" | custom-call | tf_op jit(solution)/shard_map/finish/pallas_call | solution.py:378

commit v4 on v3

--- a/solution.py
+++ b/solution.py
@@ -170,16 +170,6 @@
     put(2, dot(w_down, act[...], 1, 0))
     send(2, range(NX))
 
-    grad_rows = taken(1)
-    grad_pre = (dot(w_down, grad_rows, 0, 0) * slope[...]).astype(NARROW)
-    put(3, dot(w_up, grad_pre, 0, 0))
-    send(3, range(NX))
-
-    @pl.when(dp + 1 < n_dp)
-    def _():
-        pl.semaphore_wait(shard_sem, n_dp - 1 - dp)
-
-
     others = [lax.rem(dp + k, n_dp) for k in range(1, n_dp)]
     sends = list(to_pair)
 
@@ -230,17 +220,25 @@
         landed(i, plane if q else plane - 1, recv_sem.at[i, q]).wait()
         return got[i, pl.ds(plane_of(q) * plane, plane)].reshape(2 * plane, tok)
 
+    grad_rows = taken(1)
+    @pl.when(dp + 1 < n_dp)
+    def _():
+        pl.semaphore_wait(shard_sem, n_dp - 1 - dp)
+
+
+    mixed_down = dot(grad_rows, act[...], 1, 1).astype(NARROW)
+    part[1] = chunked(
+        jnp.concatenate([dot(pick_down[b], mixed_down[:, N * b : N * b + N], 1, 0) for b in range(2)], 0)
+    )
+    scat_down = scatter_block(1)
+    grad_pre = (dot(w_down, grad_rows, 0, 0) * slope[...]).astype(NARROW)
+    put(3, dot(w_up, grad_pre, 0, 0))
+    send(3, range(NX))
     mixed_up = dot(grad_pre, permuted, 1, 1).astype(NARROW)
     part[0] = chunked(
         jnp.concatenate([dot(mixed_up[N * b : N * b + N], pick_up[b], 1, 1) for b in range(2)], 0)
     )
     scat_up = scatter_block(0)
-    mixed_down = dot(grad_rows, act[...], 1, 1).astype(NARROW)
-    part[1] = chunked(
-        jnp.concatenate([dot(pick_down[b], mixed_down[:, N * b : N * b + N], 1, 0) for b in range(2)], 0)
-    )
-    scat_down = scatter_block(1)
-
     def to_partner(i, value):
         halves[i] = value.reshape(2, half, tok)
         halves_out[i] = halves[i, 1 - core].astype(NARROW)
@@ -266,10 +264,11 @@
         qpart[s, q] = chunked(value)
         return scatter_plane(s, q)
 
-    scat_second = [plane_grad(0, q, d_block) for q in range(NX)]
+    scat_second = [plane_grad(0, q, d_block) for q in range(2)]
+    gath_down = gather_block(1, scat_down)
+    scat_second += [plane_grad(0, q, d_block) for q in range(2, NX)]
+    gath_up = gather_block(0, scat_up)
     out_half = to_partner(0, dot(ds_ref[...], got[2].reshape(rows, tok), 0, 0))
-    gath_up = gather_block(0, scat_up)
-    gath_down = gather_block(1, scat_down)
     scat_first = [plane_grad(1, 0, x_block), plane_grad(1, 1, x_block)]
     gath_second = [gather_plane(0, q, scat_second[q]) for q in range(NX)]
     scat_first += [plane_grad(1, q, x_block) for q in range(2, NX)]

time: 56.2 us -> 55.5 us (0.988); the launches traced: 56 us -> 54.6 us
  Pallas kernels: 55.4 us -> 54 us
    pallas_call x1, Pallas kernels: 54.5 us -> 53.1 us  [shards(): pl.pallas_call(exchange, name='exchange', out_shape=(pltpu.VMEM((half, to...]
where the time goes in v4:
time: 55.5 us; the launch traced here: 54.6 us
  Pallas kernels  54 us (97%)
  between operations  0.64 us (1%)
    pallas_call x1, Pallas kernels, shards(): pl.pallas_call(exchange, name='exchange', out_shape=(pltpu.VMEM((half, to...  53.1 us

profile of v4, /device:TPU:6, one launch (start us, length us, event | category | flops | bytes accessed | tf_op | source)
XLA Modules:
  0.0 54.6 jit_solution(14175198678319144159)
XLA Ops:
  0.6 53.1 %exchange.1 = (bf16[64,512]{1,0:T(8,128)(2,1)S(1)}, bf16[64,512]{1,0:T(8,128)(2,1)S(1)}, bf16[4,4,64,128]{3,2,1,0:T(8,128)(2,1)S(1)}) custom-call(bf16[64,512]{1,0:T(8,128)(2,1)} %x_hbm.1, bf16[64,512]{1,0:T(8,128)(2,1)} %d_hbm.1, bf16[256,128]{1,0:T(8,128)(2,1)} %bitcast.4, bf16[2,128,128]{2,1,0:T(8,128)(2,1)} %us_hbm.1, bf16[2,128,128]{2,1,0:T(8,128)(2,1)} %df_hbm.1, ...), custom_call_target="tpu_custom_call" | custom-call | tf_op jit(solution)/shard_map/exchange/pallas_call | solution.py:320
  53.7 0.9 %finish.1 = (bf16[64,512]{1,0:T(8,128)(2,1)}, bf16[64,512]{1,0:T(8,128)(2,1)}, f32[1,256,128]{2,1,0:T(8,128)}, f32[2,128,128]{2,1,0:T(8,128)}, f32[2,128,128]{2,1,0:T(8,128)}, /*index=5*/f32[1,256,128]{2,1,0:T(8,128)}) custom-call(bf16[64,512]{1,0:T(8,128)(2,1)S(1)} %get-tuple-element.9.mixed_in, bf16[64,512]{1,0:T(8,128)(2,1)S(1)} %get-tuple-element.10.gtok_in, ...), custom_call_target="tpu_custom_call" | custom-call | tf_op jit(solution)/shard_map/finish/pallas_call | solution.py:377
